TPU v7x, 128 devices: a whole 4x4x4 slice. The times are simulated.
128 devices in a mesh: ctx: 8 (over x, core), wide: 16 (over z, y).
Axes of the slice: x: 4, y: 4, z: 4, core: 2. Of those that a mesh axis runs over, the one named last changes fastest.
Arguments:
- tokens: bfloat16 [16384, 2688], P(('ctx', 'wide')), may hold values from -10 to 10
- mamba_gain: float32 [2688], replicated, may hold values from 0.25 to 1.75
- w_z: bfloat16 [2688, 4096], P(None, 'wide'), may hold values from -0.125 to 0.125
- w_x: bfloat16 [2688, 4096], P(None, 'wide'), may hold values from -0.125 to 0.125
- w_bc: bfloat16 [2688, 2048], P(None, 'wide'), may hold values from -0.125 to 0.125
- w_dt: bfloat16 [2688, 64], replicated, may hold values from -1 to 1
- dt_bias: float32 [64], P('wide'), may hold values from -2 to 0
- a_log: float32 [64], P('wide')
- conv_x: float32 [4, 4096], P(None, 'wide'), may hold values from -3 to 3
- conv_bc: float32 [4, 2048], replicated, may hold values from -3 to 3
- skip: float32 [64], P('wide'), may hold values from 0.5 to 1.5
- norm_gain: float32 [4096], P('wide'), may hold values from 0.25 to 1.75
- w_out: bfloat16 [4096, 2688], P('wide'), may hold values from -0.09375 to 0.09375
- moe_gain: float32 [2688], replicated, may hold values from 0.25 to 1.75
- expert_ids: int32 [16384, 6], P(('ctx', 'wide')), may hold values from 0 to 127, all different within a row; in each aligned block of 128 rows (0 to 127, 128 to 255, ...) at most 7 rows name the same one
- router_weights: float32 [16384, 6], P(('ctx', 'wide')), may hold values from 0.05 to 0.5
- w_up: bfloat16 [128, 2688, 1856], P(('ctx', 'wide')), may hold values from -0.125 to 0.125
- w_down: bfloat16 [128, 1856, 2688], P(('ctx', 'wide')), may hold values from -0.125 to 0.125
Outputs:
- mixed: bfloat16 [16384, 2688], P(('ctx', 'wide'))
Inputs may be any that keep to these rules, and one draw needn't show every extreme that they name: `expert_ids`: within the rows of one device (128 tokens), no expert is named more than 7 times, and a row names 6 different experts.
All inputs are finite; a program needn't handle non-finite values.
Results may differ from a plain program's by a relative error of at most 0.015.
Values may be sent and summed in bfloat16 or wider, within the bound.
A program may use at most 128 MiB of HBM per device.

v0:
```python
import jax
import jax.numpy as jnp
from jax import lax
from jax.sharding import PartitionSpec as P

STATE = 128
GROUPS = 8
KERNEL = 4
TOP = 6
EXP_DEV = 1
BLOCK = 128


EPSILON = 1e-05
PRECISE = lax.Precision.HIGHEST


def partner_2(block, axis, bit):
    count = lax.axis_size(axis)
    route = []
    for low in range(count):
        high = low | 1 << bit
        if high != low and high < count:
            route += [(low, high), (high, low)]
    return lax.ppermute(block, axis, route)


def shifted(block, axis, distance):
    devices = range(lax.axis_size(axis))
    route = [(i - distance, i) for i in devices if i - distance in devices]
    return lax.ppermute(block, axis, route)


def rms_scale(values, gain_vec):
    mean_sq = jnp.mean(values * values, axis=-1, keepdims=True)
    return values * lax.rsqrt(mean_sq + EPSILON) * gain_vec


def slot_numbers(flat_ids, experts):
    onehot = (flat_ids[:, None] == jnp.arange(experts, dtype=jnp.int32)[None, :]).astype(jnp.int32)
    before = jnp.cumsum(onehot, axis=0) - onehot
    return jnp.sum(before * onehot, axis=1)


def expert_apply(arrived, w_up, w_down):
    model_width = arrived.shape[2]
    slot_count = arrived.shape[1]
    grouped = arrived.reshape(-1, EXP_DEV, slot_count, model_width)
    up_proj = jnp.einsum("secd,edf->secf", grouped, w_up, preferred_element_type=jnp.float32)
    activated = jax.nn.relu(up_proj)
    activated = (activated * activated).astype(jnp.bfloat16)
    expert_out = jnp.einsum(
        "secf,efd->secd", activated, w_down, preferred_element_type=jnp.float32
    ).astype(jnp.bfloat16)
    return expert_out.reshape(arrived.shape)


def shards(
    tokens,
    mamba_gain,
    w_z,
    w_x,
    w_bc,
    w_dt,
    dt_bias,
    a_log,
    conv_x,
    conv_bc,
    skip,
    norm_gain,
    w_out,
    moe_gain,
    expert_ids,
    router_weights,
    w_up,
    w_down,
):
    wide_count = lax.axis_size("wide")
    ctx_count = lax.axis_size("ctx")
    tok_rows, model_width = tokens.shape
    heads_here = dt_bias.shape[0]
    inner_here = w_z.shape[1]
    head_dim = inner_here // heads_here
    stream = tokens.astype(jnp.float32)
    normed = rms_scale(stream, mamba_gain).astype(jnp.bfloat16)
    merged_weight = jnp.concatenate([w_z, w_x, w_bc], 1)
    projected = jnp.dot(
        lax.all_gather(normed, "wide", axis=0, tiled=True),
        merged_weight,
        preferred_element_type=jnp.float32,
    ).astype(jnp.bfloat16)
    gate_in = projected[:, :inner_here]
    x_in = projected[:, inner_here : 2 * inner_here]
    bc_share = projected[:, 2 * inner_here :]
    raw_steps = jnp.dot(normed, w_dt, preferred_element_type=jnp.float32)
    steps_here = lax.all_to_all(raw_steps, "wide", split_axis=1, concat_axis=0, tiled=True)
    position = lax.axis_index("wide")
    members = wide_count // GROUPS
    partner = partner_2(bc_share, "wide", 0)
    upper_half = position // 2**0 % 2
    bc_share = jnp.where(
        upper_half == 1,
        jnp.concatenate([partner, bc_share], 1),
        jnp.concatenate([bc_share, partner], 1),
    )
    group_index = position // members
    taps_group = lax.dynamic_slice_in_dim(conv_bc, group_index * 2 * STATE, 2 * STATE, 1)
    pre_conv = jnp.concatenate([x_in, bc_share], 1)
    rim_rows = shifted(pre_conv[-(KERNEL - 1) :], "ctx", 1)
    extended = jnp.concatenate([rim_rows, pre_conv], 0).astype(jnp.float32)
    conv_taps = jnp.concatenate([conv_x, taps_group], 1)
    span_rows = pre_conv.shape[0]
    total = jnp.zeros(pre_conv.shape, jnp.float32)
    for offset in range(KERNEL):
        total = total + conv_taps[offset] * extended[offset : offset + span_rows]
    conved = jax.nn.silu(total)
    x_conv = conved[:, :inner_here]
    b_conv = conved[:, inner_here : inner_here + STATE]
    c_conv = conved[:, inner_here + STATE :]
    step_size = jax.nn.softplus(steps_here + dt_bias)
    log_decay = -jnp.exp(a_log) * step_size
    blocks = span_rows // BLOCK
    x_blocks = x_conv.reshape(blocks, BLOCK, heads_here, head_dim)
    b_blocks = b_conv.reshape(blocks, BLOCK, STATE)
    c_blocks = c_conv.reshape(blocks, BLOCK, STATE)
    step_blocks = step_size.reshape(blocks, BLOCK, heads_here)
    cum_decay = jnp.cumsum(log_decay.reshape(blocks, BLOCK, heads_here), axis=1)
    scores = jnp.einsum("nis,njs->nij", c_blocks, b_blocks, precision=PRECISE)
    cum_heads = jnp.transpose(cum_decay, (0, 2, 1))
    gap_decay = cum_heads[:, :, :, None] - cum_heads[:, :, None, :]
    causal = jnp.arange(BLOCK)[:, None] >= jnp.arange(BLOCK)[None, :]
    decay_mask = jnp.exp(jnp.where(causal[None, None], gap_decay, -jnp.inf))
    weights = scores[:, None] * decay_mask * jnp.transpose(step_blocks, (0, 2, 1))[:, :, None, :]
    y_intra = jnp.einsum("nhij,njhp->nihp", weights, x_blocks, precision=PRECISE)
    tail_factor = jnp.exp(cum_decay[:, -1:, :] - cum_decay) * step_blocks
    block_states = jnp.einsum(
        "njh,njhp,njs->nhps", tail_factor, x_blocks, b_blocks, precision=PRECISE
    )
    block_decay = jnp.exp(cum_decay[:, -1, :])

    def advance(carry, item):
        carried, decay_before = carry
        state_block, decay_block = item
        return (
            (decay_block[:, None, None] * carried + state_block, decay_before * decay_block),
            (carried, decay_before),
        )

    zero_state = jnp.zeros((heads_here, head_dim, STATE), jnp.float32)
    (span_state, span_decay), (starts, decays_before) = lax.scan(
        advance, (zero_state, jnp.ones((heads_here,), jnp.float32)), (block_states, block_decay)
    )

    def relay_state(turn, incoming):
        return shifted(span_decay[:, None, None] * incoming + span_state, "ctx", 1)

    incoming = lax.fori_loop(0, ctx_count - 1, relay_state, zero_state)
    starts = starts + decays_before[:, :, None, None] * incoming[None]
    y_inter = jnp.exp(cum_decay)[..., None] * jnp.einsum(
        "nis,nhps->nihp", c_blocks, starts, precision=PRECISE
    )
    y_total = (y_intra + y_inter).reshape(span_rows, heads_here, head_dim)
    y_total = y_total + skip[:, None] * x_conv.reshape(span_rows, heads_here, head_dim)
    gated = y_total * jax.nn.silu(gate_in.astype(jnp.float32)).reshape(
        span_rows, heads_here, head_dim
    )
    gated = gated * lax.rsqrt(jnp.mean(gated * gated, axis=-1, keepdims=True) + EPSILON)
    gated = (gated.reshape(span_rows, inner_here) * norm_gain).astype(jnp.bfloat16)
    mamba_out = lax.psum_scatter(
        jnp.dot(gated, w_out, preferred_element_type=jnp.float32).astype(jnp.bfloat16),
        "wide",
        scatter_dimension=0,
        tiled=True,
    ).astype(jnp.float32)
    hidden_stream = (stream + mamba_out).astype(jnp.bfloat16)
    hidden_f32 = hidden_stream.astype(jnp.float32)
    moe_in = rms_scale(hidden_f32, moe_gain).astype(jnp.bfloat16)
    experts = EXP_DEV * ctx_count * wide_count
    capacity = max(2, (7 * tok_rows * TOP + 6 * experts - 1) // (6 * experts))
    flat_ids = expert_ids.reshape(-1)
    slots = slot_numbers(flat_ids, experts)
    slot_index = flat_ids * capacity + slots
    repeated = jnp.repeat(moe_in, TOP, axis=0)
    outgoing = (
        jnp.zeros((experts * capacity, model_width), jnp.bfloat16).at[slot_index].set(repeated)
    )
    outgoing = outgoing.reshape(experts, capacity, model_width)
    returned = lax.all_to_all(
        expert_apply(
            lax.all_to_all(outgoing, ("ctx", "wide"), split_axis=0, concat_axis=0, tiled=True),
            w_up,
            w_down,
        ),
        ("ctx", "wide"),
        split_axis=0,
        concat_axis=0,
        tiled=True,
    )
    picked = returned.reshape(experts * capacity, model_width)[slot_index].reshape(
        tok_rows, TOP, model_width
    )
    combined = jnp.einsum("tk,tkd->td", router_weights, picked.astype(jnp.float32))
    return (hidden_f32 + combined).astype(jnp.bfloat16)


def solution(mesh):
    placed = (
        P(("ctx", "wide"), None),
        P(),
        P(None, "wide"),
        P(None, "wide"),
        P(None, "wide"),
        P(),
        P("wide"),
        P("wide"),
        P(None, "wide"),
        P(),
        P("wide"),
        P("wide"),
        P("wide", None),
        P(),
        P(("ctx", "wide"), None),
        P(("ctx", "wide"), None),
        P(("ctx", "wide"), None, None),
        P(("ctx", "wide"), None, None),
    )
    return jax.shard_map(
        shards, mesh=mesh, in_specs=placed, out_specs=P(("ctx", "wide"), None), check_vma=False
    )
```

profile of v0, /device:TPU:1, one launch (start us, length us, event | category | flops | bytes accessed | tf_op | source)
XLA Modules:
  0.0 597.4 jit_solution(12333369317549259145)
XLA Ops:
  6.6 1.4 fusion.65
  8.0 2.2 fusion.67
  10.3 2.1 fusion.109
  12.3 8.6 %all-to-all-start = ((f32[128,16,4]{0,2,1:T(4,128)}), f32[128,16,4]{0,2,1:T(4,128)S(1)}, u32[]{:S(2)}, u32[]{:S(2)}) async-start(f32[128,16,4]{0,2,1:T(4,128)} %bitcast.4), calls=%async_computation | async-start | bytes 65536 | tf_op jit(solution)/shard_map/all_to_all | solution.py:96
  22.0 5.4 all-to-all-done
  29.7 66.6 %all-gather.2.cloned.1.call-done = bf16[2048,2688]{1,0:T(8,128)(2,1)} async-done(((bf16[128,2688]{1,0:T(8,128)(2,1)}), bf16[2048,2688]{1,0:T(8,128)(2,1)}) %all-gather.2.cloned.1.call-update) | async-done | bytes 11010064 | tf_op jit(solution)/shard_map/all_gather | solution.py:88
  96.3 11.5 %fusion.35 = bf16[2048,640]{0,1:T(8,128)(2,1)S(1)} fusion(bf16[2048,2688]{1,0:T(8,128)(2,1)} %all-gather.2.cloned.1.call-done, bf16[2688,128]{1,0:T(8,128)(2,1)} %param.26, bf16[2688,256]{1,0:T(8,128)(2,1)} %param.25, bf16[2688,256]{1,0:T(8,128)(2,1)} %param.24), kind=kOutput, calls=%fused_computation.39 | convolution fusion | flops 7058063360 | bytes 17072128 | tf_op jit(solution)/shard_map/dot_general | solution.py:87
  107.8 1.3 collective-permute-start.1
  109.1 1.6 compare_select_fusion
  110.7 2.1 fusion.108
  112.9 7.6 %collective-permute-done.1 = bf16[2048,128]{0,1:T(8,128)(2,1)S(1)} collective-permute-done((bf16[2048,128]{0,1:T(8,128)(2,1)S(1)}, bf16[2048,128]{0,1:T(8,128)(2,1)S(1)}, u32[]{:S(2)}, u32[]{:S(2)}) %collective-permute-start.1) | collective-permute-done | bytes 524320 | tf_op jit(solution)/shard_map/ppermute | solution.py:25
  121.9 5.0 collective-permute-start.2
  127.4 1.7 copy.83
  129.1 1.6 copy.85
  130.7 1.6 copy.88
  132.4 2.3 maximum_convert_fusion
  134.6 4.1 divide_multiply_fusion
  138.9 1.7 slice_bitcast_fusion.3
  141.4 1.3 copy.114
  142.9 4.1 fusion.53
  147.0 28.2 %while.28 = (s32[]{:T(128)}, f32[4,64,128]{2,1,0:T(8,128)S(1)}, f32[4]{0:T(128)S(1)}, f32[16,4,64,128]{3,2,1,0:T(8,128)}, f32[16,4]{1,0:T(8,128)S(1)}, /*index=5...) while((s32[]{:T(128)}, f32[4,64,128]{2,1,0:T(8,128)S(1)}, ...), condition=%wide.region_3.4_spmd.clone, body=%wide.region_2.3_spmd.clone.sunk | while | flops 131083 | bytes 655617 | solution.py:150
  147.7 1.0 bitcast_add_fusion.5
  151.1 1.0 bitcast_add_fusion.5
  161.5 1.0 bitcast_add_fusion.5
  165.0 1.0 bitcast_add_fusion.5
  170.2 1.0 bitcast_add_fusion.5
  175.2 3.2 fusion.73
  178.4 10.1 %fusion.14 = f32[16,4,64,128]{3,2,1,0:T(8,128)} fusion(f32[16,4,128]{2,1,0:T(4,128)S(1)} %copy.83, f32[16,4,128]{2,1,0:T(4,128)S(1)} %copy.81, f32[16,128,128]{2,1,0:T(8,128)S(1)} %fusion.73, pred[128,128]{1,0:T(8,128)(4,1)S(1)} %iota_compare_fusion.3, f32[16,128,4,64]{1,0,3,2:T(8,128)S(1)} %bitcast.159), kind=kOutput, calls=%fused_computation.25 | convolution fusion | flops 809500672 | bytes 5324800 | tf_op jit(solution)/shard_map/nhij,njhp->nihp/dot_general | solution.py:134
  188.5 42.3 %while.27 = (s32[]{:T(128)}, f32[4,64,128]{2,1,0:T(8,128)S(1)}, f32[4]{0:T(128)S(1)}, f32[4,64,128]{2,1,0:T(8,128)S(1)}, s32[]{:T(128)}) while((s32[]{:T(128)}, f32[4,64,128]{2,1,0:T(8,128)S(1)}, f32[4]{0:T(128)S(1)}, f32[4,64,128]{2,1,0:T(8,128)S(1)}, s32[]{:T(128)}) %tuple.53), condition=%wide.region_5.6_spmd, body=%wide.region_4.5_spmd.sunk | while | flops 65538 | bytes 917621 | solution.py:157
  188.6 1.9 collective-permute-start
  190.5 1.9 collective-permute-done
  192.5 4.4 collective-permute-start
  196.9 1.9 collective-permute-done
  198.9 4.4 collective-permute-start
  203.2 1.9 collective-permute-done
  205.2 4.4 collective-permute-start
  209.6 1.9 collective-permute-done
  211.6 4.4 collective-permute-start
  216.0 1.9 collective-permute-done
  218.0 4.4 collective-permute-start
  222.3 1.9 collective-permute-done
  224.4 4.4 collective-permute-start
  228.7 1.9 collective-permute-done
  230.8 4.7 bitcast_add_fusion.3
  236.5 1.2 copy.93
  237.8 1.6 fusion.46
  239.4 5.9 convolution_convert_fusion
  247.4 88.8 %reduce-scatter.2.cloned.1.call-done = bf16[128,2688]{1,0:T(8,128)(2,1)} async-done(((bf16[2048,2688]{1,0:T(8,128)(2,1)}), bf16[128,2688]{1,0:T(8,128)(2,1)}) %reduce-scatter.2.cloned.1.call-update) | async-done | bytes 688144 | tf_op jit(solution)/shard_map/reduce_scatter | solution.py:169
  336.2 1.4 fusion.69
  337.6 1.4 fusion.71
  339.0 3.0 broadcast_in_dim.38
  342.0 7.3 %reshape.199 = bf16[768,2688]{1,0:T(8,128)(2,1)} reshape(bf16[128,6,2688]{2,1,0:T(8,128)(2,1)} %broadcast_in_dim.38) | data formatting | bytes 8257536 | tf_op jit(solution)/shard_map/reshape | solution.py:183
  349.4 12.7 %scatter_custom_fusion = bf16[896,2688]{1,0:T(8,128)(2,1)} fusion(s32[768]{0:T(1024)S(1)} %fusion.99, bf16[768,2688]{1,0:T(8,128)(2,1)} %reshape.199, bf16[]{:T(256)} %constant.98.clone.1), kind=kCustom, calls=%fused_computation.44 | custom fusion | bytes 4817408 | tf_op jit(solution)/shard_map/scatter | solution.py:185
  362.1 7.6 %reshape.182 = bf16[128,7,2688]{2,1,0:T(8,128)(2,1)} reshape(bf16[896,2688]{1,0:T(8,128)(2,1)} %scatter_custom_fusion) | data formatting | bytes 9633792 | tf_op jit(solution)/shard_map/reshape | solution.py:187
  369.6 75.2 %all_to_all.23 = bf16[128,7,2688]{2,1,0:T(8,128)(2,1)} all-to-all(bf16[128,7,2688]{2,1,0:T(8,128)(2,1)} %reshape.182), channel_id=1, replica_groups=mesh['ctx'=8,'wide'=16] {'ctx','wide'}, dimensions={0} | all-to-all | bytes 9633792 | tf_op jit(solution)/shard_map/all_to_all | solution.py:190
  444.9 33.9 %fusion.7 = bf16[128,7,2688]{2,0,1:T(8,128)(2,1)} fusion(bf16[1,1856,2688]{2,1,0:T(8,128)(2,1)} %param.39, bf16[1,2688,1856]{1,2,0:T(8,128)(2,1)} %param.38, bf16[128,7,2688]{2,1,0:T(8,128)(2,1)} %all_to_all.23), kind=kOutput, calls=%fused_computation.16 | convolution fusion | flops 17887715328 | bytes 29589504 | tf_op jit(solution)/shard_map/secf,efd->secd/dot_general | solution.py:52
  478.8 7.7 %copy.101 = bf16[128,7,2688]{2,1,0:T(8,128)(2,1)} copy(bf16[128,7,2688]{2,0,1:T(8,128)(2,1)} %fusion.7) | data formatting | bytes 9633792 | tf_op jit(solution)/shard_map/convert_element_type | solution.py:54
  486.5 6.4 %all-to-all-start.2 = ((bf16[128,7,2688]{2,1,0:T(8,128)(2,1)}), bf16[128,7,2688]{2,1,0:T(8,128)(2,1)}, u32[]{:S(2)}, u32[]{:S(2)}) async-start(bf16[128,7,2688]{2,1,0:T(8,128)(2,1)} %copy.101), calls=%async_computation.3 | async-start | bytes 11010048 | tf_op jit(solution)/shard_map/all_to_all | solution.py:188
  493.0 65.2 %all-to-all-done.2 = bf16[128,7,2688]{2,1,0:T(8,128)(2,1)} async-done(((bf16[128,7,2688]{2,1,0:T(8,128)(2,1)}), bf16[128,7,2688]{2,1,0:T(8,128)(2,1)}, u32[]{:S(2)}, u32[]{:S(2)}) %all-to-all-start.2) | async-done | bytes 4816928 | tf_op jit(solution)/shard_map/all_to_all | solution.py:188
  558.2 7.7 %reshape.185 = bf16[896,2688]{1,0:T(8,128)(2,1)} reshape(bf16[128,7,2688]{2,1,0:T(8,128)(2,1)} %all-to-all-done.2) | data formatting | bytes 9633792 | tf_op jit(solution)/shard_map/reshape | solution.py:199
  565.8 11.8 %gather_fusion = bf16[768,2688]{1,0:T(8,128)(2,1)} fusion(bf16[896,2688]{1,0:T(8,128)(2,1)} %reshape.185, s32[1024]{0:T(1024)S(1)} %pad_clamp_fusion), kind=kCustom, calls=%fused_computation | custom fusion | bytes 8260608 | tf_op jit(solution)/shard_map/gather | solution.py:199
  577.6 7.2 %reshape.186 = bf16[128,6,2688]{2,1,0:T(8,128)(2,1)} reshape(bf16[768,2688]{1,0:T(8,128)(2,1)} %gather_fusion) | data formatting | bytes 8257536 | tf_op jit(solution)/shard_map/reshape | solution.py:199
  584.8 4.3 fusion.110
  589.2 1.1 fusion.72
  (169 shorter events, 32.6 us)
Async XLA Ops:
  6.5 232.8 %copy-start = (bf16[256,2688]{1,0:T(8,128)(2,1)S(1)}, bf16[256,2688]{1,0:T(8,128)(2,1)}, u32[]{:S(2)}) copy-start(bf16[256,2688]{1,0:T(8,128)(2,1)} %param.34) | copy-start | bytes 4128772
  6.5 3.7 copy-start.17
  6.5 15.2 %copy-start.25 = (f32[4]{0:T(128)S(1)}, f32[4]{0:T(128)}, u32[]{:S(2)}) copy-start(f32[4]{0:T(128)} %param.29) | copy-start | bytes 52
  6.5 15.2 %copy-start.22 = (f32[4,256]{1,0:T(4,128)S(1)}, f32[4,256]{1,0:T(4,128)}, u32[]{:S(2)}) copy-start(f32[4,256]{1,0:T(4,128)} %param.30) | copy-start | bytes 12292
  6.5 15.3 %copy-start.23 = (f32[4]{0:T(128)S(1)}, f32[4]{0:T(128)}, u32[]{:S(2)}) copy-start(f32[4]{0:T(128)} %param.32) | copy-start | bytes 52
  6.5 89.7 %all-gather.2.cloned.1.call-start = ((), (), s32[]{:S(2)}) async-start(), calls=%async_computation.4 | async-start | bytes 11698176 | tf_op jit(solution)/shard_map/all_gather | solution.py:88
  8.0 19.9 %copy-start.20 = (f32[4]{0:T(128)S(1)}, f32[4]{0:T(128)}, u32[]{:S(2)}) copy-start(f32[4]{0:T(128)} %param.28) | copy-start | bytes 52
  12.3 15.1 %all-to-all-start = ((f32[128,16,4]{0,2,1:T(4,128)}), f32[128,16,4]{0,2,1:T(4,128)S(1)}, u32[]{:S(2)}, u32[]{:S(2)}) async-start(f32[128,16,4]{0,2,1:T(4,128)} %bitcast.4), calls=%async_computation | async-start | bytes 65536 | tf_op jit(solution)/shard_map/all_to_all | solution.py:96
  20.9 315.3 %reduce-scatter.2.cloned.1.call-start = ((), (), s32[]{:S(2)}) async-start(), calls=%async_computation.5 | async-start | bytes 11698176 | tf_op jit(solution)/shard_map/reduce_scatter | solution.py:169
  28.6 1.0 copy-start.5
  107.8 5.0 copy-start.14
  107.8 2.9 copy-start.6
  107.8 12.7 %collective-permute-start.1 = (bf16[2048,128]{0,1:T(8,128)(2,1)S(1)}, bf16[2048,128]{0,1:T(8,128)(2,1)S(1)}, u32[]{:S(2)}, u32[]{:S(2)}) collective-permute-start(bf16[2048,128]{0,1:T(8,128)(2,1)S(1)} %slice.78), channel_id=1, source_target_pairs={{0,1},{1,0},{2,3},{3,2},{4,5},{5,4},{6,7},{7,6},{8,9},{9,8},{10,11... | collective-permute-start | bytes 1572872 | tf_op jit(solution)/shard_map/ppermute | solution.py:25
  112.9 8.0 %copy-start.8 = (bf16[2048,256]{0,1:T(8,128)(2,1)}, bf16[2048,256]{0,1:T(8,128)(2,1)S(1)}, u32[]{:S(2)}) copy-start(bf16[2048,256]{0,1:T(8,128)(2,1)S(1)} %slice.77) | copy-start | bytes 3145732
  112.9 14.0 %copy-start.7 = (f32[16,128,4]{2,0,1:T(8,128)S(1)}, f32[16,128,4]{2,0,1:T(8,128)}, u32[]{:S(2)}) copy-start(f32[16,128,4]{2,0,1:T(8,128)} %copy-done.5) | copy-start | bytes 98308
  120.9 1.0 copy-start.10
  121.9 10.5 %collective-permute-start.2 = (bf16[3,512]{0,1:T(8,128)(2,1)S(1)}, bf16[3,512]{0,1:T(8,128)(2,1)S(1)}, u32[]{:S(2)}, u32[]{:S(2)}) collective-permute-start(bf16[3,512]{0,1:T(8,128)(2,1)S(1)} %pad_maximum_fusion), channel_id=1, source_target_pairs={{0,16},{16,32},{32,48},{48,64},{64,80},{80,96},{96,112},{1,17},{17... | collective-permute-start | bytes 9224 | tf_op jit(solution)/shard_map/ppermute | solution.py:31
  127.4 5.0 copy-start.9
  138.7 2.3 copy-start.2
  141.4 5.6 copy-start.11
  175.2 3.2 copy-start.12
  178.4 52.4 %copy-start.16 = (f32[16,8,16,128]{3,2,1,0:T(8,128)S(1)}, f32[16,8,16,128]{3,2,1,0:T(8,128)}, u32[]{:S(2)}) copy-start(f32[16,8,16,128]{3,2,1,0:T(8,128)} %copy.114) | copy-start | bytes 3145732
  188.6 3.9 collective-permute-start
  192.5 6.3 %collective-permute-start = (f32[4,64,128]{2,1,0:T(8,128)S(1)}, f32[4,64,128]{2,1,0:T(8,128)S(1)}, u32[]{:S(2)}, u32[]{:S(2)}) collective-permute-start(f32[4,64,128]{2,1,0:T(8,128)S(1)} %multiply_add_fusion.2), channel_id=1, source_target_pairs={{0,16},{16,32},{32,48},{48,64},{64,80},{80,96},{96,112},{1,17},{17... | collective-permute-start | bytes 393224 | tf_op jit(solution)/shard_map/while/body/eval_jaxpr/ppermute | solution.py:31
  198.9 6.3 %collective-permute-start = (f32[4,64,128]{2,1,0:T(8,128)S(1)}, f32[4,64,128]{2,1,0:T(8,128)S(1)}, u32[]{:S(2)}, u32[]{:S(2)}) collective-permute-start(f32[4,64,128]{2,1,0:T(8,128)S(1)} %multiply_add_fusion.2), channel_id=1, source_target_pairs={{0,16},{16,32},{32,48},{48,64},{64,80},{80,96},{96,112},{1,17},{17... | collective-permute-start | bytes 393224 | tf_op jit(solution)/shard_map/while/body/eval_jaxpr/ppermute | solution.py:31
  205.2 6.3 %collective-permute-start = (f32[4,64,128]{2,1,0:T(8,128)S(1)}, f32[4,64,128]{2,1,0:T(8,128)S(1)}, u32[]{:S(2)}, u32[]{:S(2)}) collective-permute-start(f32[4,64,128]{2,1,0:T(8,128)S(1)} %multiply_add_fusion.2), channel_id=1, source_target_pairs={{0,16},{16,32},{32,48},{48,64},{64,80},{80,96},{96,112},{1,17},{17... | collective-permute-start | bytes 393224 | tf_op jit(solution)/shard_map/while/body/eval_jaxpr/ppermute | solution.py:31
  211.6 6.3 %collective-permute-start = (f32[4,64,128]{2,1,0:T(8,128)S(1)}, f32[4,64,128]{2,1,0:T(8,128)S(1)}, u32[]{:S(2)}, u32[]{:S(2)}) collective-permute-start(f32[4,64,128]{2,1,0:T(8,128)S(1)} %multiply_add_fusion.2), channel_id=1, source_target_pairs={{0,16},{16,32},{32,48},{48,64},{64,80},{80,96},{96,112},{1,17},{17... | collective-permute-start | bytes 393224 | tf_op jit(solution)/shard_map/while/body/eval_jaxpr/ppermute | solution.py:31
  218.0 6.3 %collective-permute-start = (f32[4,64,128]{2,1,0:T(8,128)S(1)}, f32[4,64,128]{2,1,0:T(8,128)S(1)}, u32[]{:S(2)}, u32[]{:S(2)}) collective-permute-start(f32[4,64,128]{2,1,0:T(8,128)S(1)} %multiply_add_fusion.2), channel_id=1, source_target_pairs={{0,16},{16,32},{32,48},{48,64},{64,80},{80,96},{96,112},{1,17},{17... | collective-permute-start | bytes 393224 | tf_op jit(solution)/shard_map/while/body/eval_jaxpr/ppermute | solution.py:31
  224.4 6.3 %collective-permute-start = (f32[4,64,128]{2,1,0:T(8,128)S(1)}, f32[4,64,128]{2,1,0:T(8,128)S(1)}, u32[]{:S(2)}, u32[]{:S(2)}) collective-permute-start(f32[4,64,128]{2,1,0:T(8,128)S(1)} %multiply_add_fusion.2), channel_id=1, source_target_pairs={{0,16},{16,32},{32,48},{48,64},{64,80},{80,96},{96,112},{1,17},{17... | collective-permute-start | bytes 393224 | tf_op jit(solution)/shard_map/while/body/eval_jaxpr/ppermute | solution.py:31
  230.8 4.7 copy-start.3
  230.8 4.7 copy-start.15
  236.5 1.3 copy-start.24
  245.3 0.7 copy-start.18
  246.0 90.2 %copy-start.4 = (bf16[128,2688]{1,0:T(8,128)(2,1)S(1)}, bf16[128,2688]{1,0:T(8,128)(2,1)}, u32[]{:S(2)}) copy-start(bf16[128,2688]{1,0:T(8,128)(2,1)} %param.22) | copy-start | bytes 2064388
  246.6 91.0 %copy-start.19 = (f32[2688]{0:T(1024)S(1)}, f32[2688]{0:T(1024)}, u32[]{:S(2)}) copy-start(f32[2688]{0:T(1024)} %param.35) | copy-start | bytes 32260
  486.5 6.4 %copy-start.21 = (f32[128,6]{0,1:T(8,128)S(1)}, f32[128,6]{0,1:T(8,128)}, u32[]{:S(2)}) copy-start(f32[128,6]{0,1:T(8,128)} %param.37) | copy-start | bytes 9220
  486.5 71.7 %all-to-all-start.2 = ((bf16[128,7,2688]{2,1,0:T(8,128)(2,1)}), bf16[128,7,2688]{2,1,0:T(8,128)(2,1)}, u32[]{:S(2)}, u32[]{:S(2)}) async-start(bf16[128,7,2688]{2,1,0:T(8,128)(2,1)} %copy.101), calls=%async_computation.3 | async-start | bytes 11010048 | tf_op jit(solution)/shard_map/all_to_all | solution.py:188
  584.8 4.4 copy-start.13
  584.8 5.5 copy-start.1
Sparse Core Ops, SparseCore 0:
  10.4 85.8 all-gather.1
  245.4 90.7 reduce-scatter.1
where the time goes:
time: 606 us; the launch traced here: 597 us
  waiting for transfers between devices  247 us (41%)
  local copies, waits for them, and re-layouts  81.8 us (13%)
  matrix products  79.7 us (13%)
  blocking collectives  75.2 us (12%)
  starting transfers between devices  49.3 us (8%)
  other arithmetic  48.9 us (8%)
  between operations  14.2 us (2%)
    reduce_scatter x1, waiting for transfers between devices, shards(): lax.psum_scatter(jnp.dot(gated, w_out, preferred_element_type=jnp.float32...  88.8 us
    all_to_all x1, blocking collectives, shards(): lax.all_to_all(outgoing, ('ctx', 'wide'), split_axis=0, concat_axis=0, ti...  75.2 us
    all_gather x1, waiting for transfers between devices, shards(): lax.all_gather(normed, 'wide', axis=0, tiled=True)  66.6 us
    all_to_all x1, waiting for transfers between devices, shards(): lax.all_to_all(expert_apply(lax.all_to_all(outgoing, ('ctx', 'wide'), spl...  65.2 us
    dot_general x1, matrix products, expert_apply(): jnp.einsum('secf,efd->secd', activated, w_down, preferred_element_type=jn...  33.9 us
    ppermute x8, starting transfers between devices, shifted(): return lax.ppermute(block, axis, route)  33 us
    add x16, other arithmetic, advance(): decay_block[:, None, None] * carried + state_block  15.7 us
    reshape x2, local copies, waits for them, and re-layouts, shards(): returned.reshape(experts * capacity, model_width)[slot_index]  14.9 us
  transfers between devices with their start and end apart: 13, of which 12 were waited for; matrix products, arithmetic and copies ran while one was open for 3% of the time, Pallas kernels for 0%

commit v1 on v0

v1 whole, which is shorter than its diff:
```python
import functools

import jax
import jax.numpy as jnp
from jax import lax
from jax.experimental import pallas as pl
from jax.experimental.pallas import tpu as pltpu
from jax.sharding import PartitionSpec as P

STATE = 128
GROUPS = 8
KERNEL = 4
TOP = 6
BLOCK = 128
HEAD_DIM = 64
RIM = 8

EPSILON = 1e-05
PRECISE = lax.Precision.HIGHEST
BF16 = jnp.bfloat16
F32 = jnp.float32


def shifted(block, axis, distance):
    devices = range(lax.axis_size(axis))
    route = [(i - distance, i) for i in devices if i - distance in devices]
    return lax.ppermute(block, axis, route)


def rms_scale(values, gain_vec):
    mean_sq = jnp.mean(values * values, axis=-1, keepdims=True)
    return values * lax.rsqrt(mean_sq + EPSILON) * gain_vec


def by_head(columns, width):
    rows, heads = columns.shape
    lane_head = lax.broadcasted_iota(jnp.int32, (rows, width), 1) // HEAD_DIM
    out = jnp.broadcast_to(columns[:, 0:1], (rows, width))
    for h in range(1, heads):
        out = jnp.where(lane_head == h, columns[:, h : h + 1], out)
    return out


def scan_kernel(
    heads, proj_ref, rim_ref, taps_ref, skip_ref, steps_ref, steps_t_ref,
    y_ref, c_ref, cum_ref, state_ref, ext, running,
):
    n = pl.program_id(0)
    width = heads * HEAD_DIM
    columns = width + 2 * STATE

    @pl.when(n == 0)
    def _():
        ext[0:RIM, :] = rim_ref[...].astype(F32)
        state_ref[...] = jnp.zeros_like(state_ref)
        running[...] = jnp.zeros_like(running)

    @pl.when(n > 0)
    def _():
        ext[0:RIM, :] = ext[BLOCK : BLOCK + RIM, :]

    ext[RIM : RIM + BLOCK, :] = proj_ref[:, width:].astype(F32)
    total = jnp.zeros((BLOCK, columns), F32)
    for tap in range(KERNEL):
        start = RIM - (KERNEL - 1) + tap
        total = total + taps_ref[tap : tap + 1, :] * ext[start : start + BLOCK, :]
    conved = total * jax.nn.sigmoid(total)
    x = conved[:, :width]
    b = conved[:, width : width + STATE].astype(BF16)
    c = conved[:, width + STATE :].astype(BF16)

    row = lax.broadcasted_iota(jnp.int32, (BLOCK, BLOCK), 0)
    col = lax.broadcasted_iota(jnp.int32, (BLOCK, BLOCK), 1)
    causal = row >= col
    lower = causal.astype(F32)
    upper = (row <= col).astype(F32)
    steps = steps_ref[...]
    cum = jnp.dot(lower, steps, precision=PRECISE, preferred_element_type=F32)
    cum_t = jnp.dot(steps_t_ref[...], upper, precision=PRECISE, preferred_element_type=F32)
    decay = cum[:, heads : 2 * heads]
    x_step = x * by_head(steps[:, :heads], width)
    x_bf = x_step.astype(BF16)
    scores = lax.dot_general(c, b, (((1,), (1,)), ((), ())), preferred_element_type=F32)
    lane_head = lax.broadcasted_iota(jnp.int32, (BLOCK, width), 1) // HEAD_DIM
    y = None
    for h in range(heads):
        gap = decay[:, h : h + 1] - cum_t[heads + h : heads + h + 1, :]
        weight = scores * jnp.exp(jnp.where(causal, gap, -jnp.inf))
        part = jnp.dot(weight.astype(BF16), x_bf, preferred_element_type=F32)
        y = part if y is None else jnp.where(lane_head == h, part, y)
    state = state_ref[...]
    y = y + by_head(jnp.exp(decay), width) * jnp.dot(
        c, state.astype(BF16), preferred_element_type=F32
    )
    y_ref[...] = y + skip_ref[...] * x
    c_ref[...] = c
    last = decay[BLOCK - 1 : BLOCK, :]
    tail = (x_step * by_head(jnp.exp(last - decay), width)).astype(BF16)
    state_ref[...] = by_head(jnp.exp(last), width) * state + lax.dot_general(
        b, tail, (((0,), (0,)), ((), ())), preferred_element_type=F32
    )
    span_cum = cum + running[0:1, :]
    cum_ref[...] = span_cum
    running[...] = jnp.broadcast_to(span_cum[BLOCK - 1 : BLOCK, :], running.shape)


def scan_blocks(projected, rim, taps, skip_row, steps, steps_t, heads):
    rows = projected.shape[0]
    width = heads * HEAD_DIM
    blocks = rows // BLOCK
    return pl.pallas_call(
        functools.partial(scan_kernel, heads),
        grid=(blocks,),
        in_specs=[
            pl.BlockSpec((BLOCK, projected.shape[1]), lambda n: (n, 0)),
            pl.BlockSpec(rim.shape, lambda n: (0, 0)),
            pl.BlockSpec(taps.shape, lambda n: (0, 0)),
            pl.BlockSpec(skip_row.shape, lambda n: (0, 0)),
            pl.BlockSpec((BLOCK, 2 * heads), lambda n: (n, 0)),
            pl.BlockSpec((2 * heads, BLOCK), lambda n: (0, n)),
        ],
        out_specs=[
            pl.BlockSpec((BLOCK, width), lambda n: (n, 0)),
            pl.BlockSpec((BLOCK, STATE), lambda n: (n, 0)),
            pl.BlockSpec((BLOCK, 2 * heads), lambda n: (n, 0)),
            pl.BlockSpec((STATE, width), lambda n: (0, 0)),
        ],
        out_shape=[
            jax.ShapeDtypeStruct((rows, width), F32),
            jax.ShapeDtypeStruct((rows, STATE), BF16),
            jax.ShapeDtypeStruct((rows, 2 * heads), F32),
            jax.ShapeDtypeStruct((STATE, width), F32),
        ],
        scratch_shapes=[
            pltpu.VMEM((RIM + BLOCK, width + 2 * STATE), F32),
            pltpu.VMEM((8, 2 * heads), F32),
        ],
        cost_estimate=pl.CostEstimate(
            flops=blocks * 2 * BLOCK * BLOCK * width * 7, bytes_accessed=rows * 4000,
            transcendentals=rows * 1000,
        ),
        name="scan_blocks",
    )(projected, rim, taps, skip_row, steps, steps_t)


def finish_rows(heads, y, c, cum, gate, incoming, gain):
    width = heads * HEAD_DIM
    decay = jnp.exp(cum[:, heads : 2 * heads])
    y = y + by_head(decay, width) * jnp.dot(c, incoming, preferred_element_type=F32)
    gate = gate.astype(F32)
    gated = y * (gate * jax.nn.sigmoid(gate))
    square = gated * gated
    lane_head = lax.broadcasted_iota(jnp.int32, square.shape, 1) // HEAD_DIM
    means = [
        jnp.sum(jnp.where(lane_head == h, square, 0.0), axis=1, keepdims=True) for h in range(heads)
    ]
    mean_sq = by_head(jnp.concatenate(means, axis=1), width) * (1.0 / HEAD_DIM)
    return (gated * lax.rsqrt(mean_sq + EPSILON) * gain).astype(BF16)


def finish_kernel(heads, y_ref, c_ref, cum_ref, gate_ref, incoming_ref, gain_ref, w_ref, out_ref):
    gated = finish_rows(
        heads, y_ref[...], c_ref[...], cum_ref[...], gate_ref[...], incoming_ref[...], gain_ref[...]
    )
    out_ref[...] = jnp.dot(gated, w_ref[...], preferred_element_type=F32).astype(BF16)


def finish_blocks(y, c, cum, projected, incoming, gain_row, w_out, heads):
    rows, width = y.shape
    model_width = w_out.shape[1]
    blocks = rows // BLOCK
    return pl.pallas_call(
        functools.partial(finish_kernel, heads),
        grid=(blocks,),
        in_specs=[
            pl.BlockSpec((BLOCK, width), lambda n: (n, 0)),
            pl.BlockSpec((BLOCK, STATE), lambda n: (n, 0)),
            pl.BlockSpec((BLOCK, 2 * heads), lambda n: (n, 0)),
            pl.BlockSpec((BLOCK, width), lambda n: (n, 0)),
            pl.BlockSpec(incoming.shape, lambda n: (0, 0)),
            pl.BlockSpec(gain_row.shape, lambda n: (0, 0)),
            pl.BlockSpec(w_out.shape, lambda n: (0, 0)),
        ],
        out_specs=pl.BlockSpec((BLOCK, model_width), lambda n: (n, 0)),
        out_shape=jax.ShapeDtypeStruct((rows, model_width), BF16),
        cost_estimate=pl.CostEstimate(
            flops=2 * rows * width * model_width, bytes_accessed=rows * (model_width * 2 + 2000),
            transcendentals=rows * width,
        ),
        name="finish_blocks",
    )(y, c, cum, projected, incoming, gain_row, w_out)


def route_tables(expert_ids, router_weights, experts, slots):
    tok_rows = expert_ids.shape[0]
    named = expert_ids[:, :, None] == jnp.arange(experts, dtype=jnp.int32)[None, None, :]
    member = jnp.sum(named.astype(F32), axis=1)
    weight = jnp.sum(jnp.where(named, router_weights[:, :, None], 0.0), axis=1)
    strictly = jnp.arange(tok_rows)[:, None] > jnp.arange(tok_rows)[None, :]
    before = jnp.dot(strictly.astype(BF16), member.astype(BF16), preferred_element_type=F32)
    place = jnp.where(member > 0, before, -1.0)
    slot = jnp.arange(slots, dtype=F32)
    hit = place[:, :, None] == slot[None, None, :]
    combine = jnp.where(hit, weight[:, :, None], 0.0).reshape(tok_rows, experts * slots)
    hit_t = place.T[:, None, :] == slot[None, :, None]
    dispatch = hit_t.astype(BF16).reshape(experts * slots, tok_rows)
    high = combine.astype(BF16)
    low = (combine - high.astype(F32)).astype(BF16)
    return dispatch, high, low


def shards(
    tokens,
    mamba_gain,
    w_z,
    w_x,
    w_bc,
    w_dt,
    dt_bias,
    a_log,
    conv_x,
    conv_bc,
    skip,
    norm_gain,
    w_out,
    moe_gain,
    expert_ids,
    router_weights,
    w_up,
    w_down,
):
    wide_count = lax.axis_size("wide")
    ctx_count = lax.axis_size("ctx")
    tok_rows, model_width = tokens.shape
    heads = dt_bias.shape[0]
    width = heads * HEAD_DIM
    position = lax.axis_index("wide")
    ctx_position = lax.axis_index("ctx")

    experts = ctx_count * wide_count
    capacity = max(2, (7 * tok_rows * TOP + 6 * experts - 1) // (6 * experts))
    slots = -(-capacity // 8) * 8
    dispatch, combine_high, combine_low = route_tables(expert_ids, router_weights, experts, slots)

    stream = tokens.astype(F32)
    normed = rms_scale(stream, mamba_gain).astype(BF16)
    partner_route = [(i, i ^ 1) for i in range(wide_count)]
    partner_bc = lax.ppermute(w_bc, "wide", partner_route)
    upper_half = position % 2 == 1
    weight = jnp.concatenate(
        [w_z, w_x, jnp.where(upper_half, partner_bc, w_bc), jnp.where(upper_half, w_bc, partner_bc)],
        1,
    )
    raw_steps = jnp.dot(normed, w_dt, preferred_element_type=F32)
    steps_here = lax.all_to_all(raw_steps, "wide", split_axis=1, concat_axis=0, tiled=True)
    step_size = jax.nn.softplus(steps_here + dt_bias)
    steps = jnp.concatenate([step_size, -jnp.exp(a_log) * step_size], 1)
    group_index = position // (wide_count // GROUPS)
    taps_group = lax.dynamic_slice_in_dim(conv_bc, group_index * 2 * STATE, 2 * STATE, 1)
    taps = jnp.concatenate([conv_x, taps_group], 1)

    projected = jnp.dot(
        lax.all_gather(normed, "wide", axis=0, tiled=True), weight, preferred_element_type=F32
    ).astype(BF16)
    rim = shifted(projected[-RIM:, width:], "ctx", 1)
    skip_row = jnp.repeat(skip, HEAD_DIM)[None, :]
    y, c, cum, span_state = scan_blocks(
        projected, rim, taps, skip_row, steps, steps.T, heads
    )

    span_decay = cum[-1, heads:]
    packed = jnp.concatenate(
        [span_state, jnp.broadcast_to(jnp.repeat(span_decay, HEAD_DIM)[None, :], (8, width))], 0
    )
    spans = lax.all_gather(packed, "ctx", axis=0)
    states = spans[:, :STATE]
    decays = spans[:, STATE]
    index = jnp.arange(ctx_count)
    between = (index[None, :] > index[:, None]) & (index[None, :] < ctx_position)
    gap = jnp.sum(jnp.where(between[:, :, None], decays[None, :, :], 0.0), axis=1)
    factor = jnp.where((index < ctx_position)[:, None], jnp.exp(gap), 0.0)
    incoming = jnp.sum(factor[:, None, :] * states, axis=0).astype(BF16)

    partial_out = finish_blocks(
        y, c, cum, projected, incoming, norm_gain[None, :], w_out, heads
    )
    mamba_out = lax.psum_scatter(
        partial_out, "wide", scatter_dimension=0, tiled=True
    ).astype(F32)
    hidden_stream = (stream + mamba_out).astype(BF16)
    hidden_f32 = hidden_stream.astype(F32)
    moe_in = rms_scale(hidden_f32, moe_gain).astype(BF16)

    outgoing = jnp.dot(dispatch, moe_in, preferred_element_type=F32).astype(BF16)
    arrived = lax.all_to_all(
        outgoing.reshape(experts, slots, model_width),
        ("ctx", "wide"), split_axis=0, concat_axis=0, tiled=True,
    ).reshape(experts * slots, model_width)
    up_proj = jnp.dot(arrived, w_up[0], preferred_element_type=F32)
    activated = jax.nn.relu(up_proj)
    activated = (activated * activated).astype(BF16)
    expert_out = jnp.dot(activated, w_down[0], preferred_element_type=F32).astype(BF16)
    returned = lax.all_to_all(
        expert_out.reshape(experts, slots, model_width),
        ("ctx", "wide"), split_axis=0, concat_axis=0, tiled=True,
    ).reshape(experts * slots, model_width)
    combined = jnp.dot(combine_high, returned, preferred_element_type=F32) + jnp.dot(
        combine_low, returned, preferred_element_type=F32
    )
    return (hidden_f32 + combined).astype(BF16)


def solution(mesh):
    placed = (
        P(("ctx", "wide"), None),
        P(),
        P(None, "wide"),
        P(None, "wide"),
        P(None, "wide"),
        P(),
        P("wide"),
        P("wide"),
        P(None, "wide"),
        P(),
        P("wide"),
        P("wide"),
        P("wide", None),
        P(),
        P(("ctx", "wide"), None),
        P(("ctx", "wide"), None),
        P(("ctx", "wide"), None, None),
        P(("ctx", "wide"), None, None),
    )
    return jax.shard_map(
        shards, mesh=mesh, in_specs=placed, out_specs=P(("ctx", "wide"), None), check_vma=False
    )
```

time: 606 us -> 467 us (0.77); the launches traced: 597 us -> 465 us
  local copies, waits for them, and re-layouts: 81.8 us -> 6.58 us
  blocking collectives: 75.2 us -> 147 us
  waiting for transfers between devices: 247 us -> 182 us
  starting transfers between devices: 49.3 us -> 13.6 us
  other arithmetic: 48.9 us -> 13.5 us
  Pallas kernels: 0 us -> 33.5 us
  matrix products: 79.7 us -> 55.1 us
    all_to_all x1 -> x2, blocking collectives: 75.2 us -> 147 us  [the longest x1 75 us: shards(): lax.all_to_all(outgoing.reshape(experts, slots, model_width), ('ctx', 'wi...]
    all_to_all x1 -> x0, waiting for transfers between devices: 65.2 us -> none  [shards(): lax.all_to_all(expert_apply(lax.all_to_all(outgoing, ('ctx', 'wide'), spl...]
    pallas_call x0 -> x2, Pallas kernels: none -> 33.5 us  [the longest x1 17.7 us: finish_blocks(): pl.pallas_call(functools.partial(finish_kernel, heads), grid=(blocks,), i...]
    reshape x4 -> x0, local copies, waits for them, and re-layouts: 29.8 us -> none  [the longest x2 14.9 us: shards(): returned.reshape(experts * capacity, model_width)[slot_index]]
    ppermute x8 -> x1, starting transfers between devices: 33 us -> 3.82 us  [shifted(): return lax.ppermute(block, axis, route)]
    dot_general x9 -> x7, matrix products: 79.7 us -> 55.1 us  [the longest x1 33.5 us: shards(): jnp.dot(activated, w_down[0], preferred_element_type=F32).astype(BF16)]
    all_gather x0 -> x1, waiting for transfers between devices: none -> 22.7 us  [shards(): spans = lax.all_gather(packed, 'ctx', axis=0)]
    add x23 -> x0, other arithmetic: 16.3 us -> none  [the longest x16 15.7 us: advance(): decay_block[:, None, None] * carried + state_block]
  transfers between devices with their start and end apart: 13 -> 6, of which waited for: 12 -> 4; matrix products, arithmetic and copies ran while one was open for 3% -> 2% of each run, Pallas kernels for 0% -> 0%
where the time goes in v1:
time: 467 us; the launch traced here: 465 us
  waiting for transfers between devices  182 us (39%)
  blocking collectives  147 us (31%)
  matrix products  55.1 us (12%)
  Pallas kernels  33.5 us (7%)
  starting transfers between devices  13.6 us (3%)
  other arithmetic  13.5 us (3%)
  between operations  13.3 us (3%)
  local copies, waits for them, and re-layouts  6.58 us (1%)
    reduce_scatter x1, waiting for transfers between devices, shards(): lax.psum_scatter(partial_out, 'wide', scatter_dimension=0, tiled=True)  88.7 us
    all_to_all x1, blocking collectives, shards(): lax.all_to_all(outgoing.reshape(experts, slots, model_width), ('ctx', 'wi...  75 us
    all_to_all x1, blocking collectives, shards(): lax.all_to_all(expert_out.reshape(experts, slots, model_width), ('ctx', '...  72.2 us
    all_gather x1, waiting for transfers between devices, shards(): lax.all_gather(normed, 'wide', axis=0, tiled=True)  59.8 us
    dot_general x1, matrix products, shards(): jnp.dot(activated, w_down[0], preferred_element_type=F32).astype(BF16)  33.5 us
    all_gather x1, waiting for transfers between devices, shards(): spans = lax.all_gather(packed, 'ctx', axis=0)  22.7 us
    pallas_call x1, Pallas kernels, finish_blocks(): pl.pallas_call(functools.partial(finish_kernel, heads), grid=(blocks,), i...  17.7 us
    pallas_call x1, Pallas kernels, scan_blocks(): pl.pallas_call(functools.partial(scan_kernel, heads), grid=(blocks,), in_...  15.9 us
  transfers between devices with their start and end apart: 6, of which 4 were waited for; matrix products, arithmetic and copies ran while one was open for 2% of the time, Pallas kernels for 0%

profile of v1, /device:TPU:1, one launch (start us, length us, event | category | flops | bytes accessed | tf_op | source)
XLA Modules:
  0.0 465.0 jit_solution(9413795634623903517)
XLA Ops:
  6.5 0.0 copy-start
  6.5 0.0 copy-start.5
  6.5 0.0 all-gather.4.cloned.1.call-start
  6.5 1.4 fusion.51
  8.0 2.2 fusion.53
  10.1 0.0 all-gather.4.cloned.1.call-update
  10.2 2.2 collective-permute-start
  12.4 0.0 copy-done
  12.4 2.1 fusion.80
  14.4 7.5 %all-to-all-start = ((f32[128,16,4]{0,2,1:T(4,128)}), f32[128,16,4]{0,2,1:T(4,128)S(1)}, u32[]{:S(2)}, u32[]{:S(2)}) async-start(f32[128,16,4]{0,2,1:T(4,128)} %bitcast), calls=%async_computation | async-start | bytes 65536 | tf_op jit(solution)/shard_map/all_to_all | solution.py:255
  21.9 0.0 all-gather.6.cloned.1.call-start
  22.0 0.7 exponential_negate_fusion
  22.6 0.7 constant_dynamic-slice_fusion
  23.3 1.3 pad_maximum_fusion.2.taps_ref
  24.6 0.7 broadcast_in_dim.100
  25.3 0.6 broadcast_in_dim_reshape.4.skip_ref
  26.0 11.0 %all-to-all-done = f32[128,16,4]{0,2,1:T(4,128)S(1)} async-done(((f32[128,16,4]{0,2,1:T(4,128)}), f32[128,16,4]{0,2,1:T(4,128)S(1)}, u32[]{:S(2)}, u32[]{:S(2)}) %all-to-all-start) | async-done | bytes 32800 | tf_op jit(solution)/shard_map/all_to_all | solution.py:255
  36.9 0.8 broadcast_multiply_fusion
  37.7 0.0 collective-permute-done
  37.7 0.0 copy-done.5
  37.7 1.2 broadcast_select_fusion.1
  38.9 59.8 %all-gather.4.cloned.1.call-done = bf16[2048,2688]{1,0:T(8,128)(2,1)} async-done(((bf16[128,2688]{1,0:T(8,128)(2,1)}), bf16[2048,2688]{1,0:T(8,128)(2,1)}) %all-gather.4.cloned.1.call-update) | async-done | bytes 11010064 | tf_op jit(solution)/shard_map/all_gather | solution.py:263
  98.7 13.0 %fusion.48.proj_ref.gate_ref = bf16[2048,768]{1,0:T(8,128)(2,1)S(1)} fusion(bf16[2048,2688]{1,0:T(8,128)(2,1)} %all-gather.4.cloned.1.call-done, bf16[2688,128]{1,0:T(8,128)(2,1)} %get-tuple-element.18, bf16[2688,128]{1,0:T(8,128)(2,1)} %get-tuple-element.17, bf16[2688,256]{1,0:T(8,128)(2,1)} %param.21, bf16[2688,256]{1,0:T(8,128)(2,1)} %param.20), kind=kOutput, calls=%fused_computation.28 | convolution fusion | flops 8473804800 | bytes 18284544 | tf_op jit(solution)/shard_map/dot_general | solution.py:262
  111.7 0.0 copy-start.2
  111.7 3.8 collective-permute-start.1
  115.6 0.6 fusion.78
  116.2 1.3 copy.37.steps_ref
  117.5 0.0 collective-permute-done.1.rim_ref
  117.5 0.0 copy-done.2
  117.5 0.6 copy-done.7
  118.1 15.9 %scan_blocks.1 = (f32[2048,256]{1,0:T(8,128)}, bf16[2048,128]{1,0:T(8,128)(2,1)}, f32[2048,8]{1,0:T(8,128)}, f32[128,256]{1,0:T(8,128)}) custom-call(bf16[2048,768]{1,0:T(8,128)(2,1)} %copy-done.2, bf16[8,512]{1,0:T(8,128)(2,1)} %copy-done.7, f32[4,512]{1,0:T(4,128)} %pad_maximum_fusion.2.taps_ref, f32[1,256]{1,0:T(1,128)} %broadcast_in_dim_reshape.4.skip_ref, ...), custom_call_target="tpu_custom_call" | custom-call | flops 939524096 | bytes 8192000 | tf_op jit(solution)/shard_map/scan_blocks/pallas_call | solution.py:111
  134.0 0.7 slice_bitcast_fusion
  134.7 0.1 broadcast_in_dim.103
  134.8 0.1 broadcast_in_dim.104
  134.9 1.6 pad_maximum_fusion
  136.5 0.0 all-gather.6.cloned.1.call-update
  136.5 0.0 reduce-scatter.2.cloned.1.call-start
  136.6 22.7 %all-gather.6.cloned.1.call-done = f32[1088,256]{1,0:T(8,128)} async-done(((f32[136,256]{1,0:T(8,128)}), f32[1088,256]{1,0:T(8,128)}) %all-gather.6.cloned.1.call-update) | async-done | bytes 1114128 | tf_op jit(solution)/shard_map/all_gather | solution.py:275
  159.3 0.8 slice.17
  160.1 0.1 select_reduce_fusion.1
  160.2 0.1 exponential_select_fusion
  160.3 1.9 fusion.58.incoming_ref
  162.2 17.7 %finish_blocks.1 = bf16[2048,2688]{1,0:T(8,128)(2,1)} custom-call(f32[2048,256]{1,0:T(8,128)} %get-tuple-element.9.y_ref, bf16[2048,128]{1,0:T(8,128)(2,1)} %get-tuple-element.10.c_ref, f32[2048,8]{1,0:T(8,128)} %get-tuple-element.11.cum_ref, bf16[2048,768]{1,0:T(8,128)(2,1)} %copy-done.2, bf16[128,256]{1,0:T(8,128)(2,1)} %fusion.58.incoming_ref, ...), custom_call_target="tpu_custom_call" | custom-call | flops 2818572288 | bytes 15106048 | tf_op jit(solution)/shard_map/finish_blocks/pallas_call | solution.py:172
  179.9 0.0 copy-start.3
  179.9 0.0 copy-start.6
  179.9 0.0 reduce-scatter.2.cloned.1.call-update
  180.0 0.6 copy-done.8
  180.6 0.0 copy-done.9
  180.6 0.3 select_reduce_fusion
  180.9 0.1 convolution_select_fusion
  181.0 0.1 copy.38
  181.1 0.1 eq.64
  181.2 88.7 %reduce-scatter.2.cloned.1.call-done = bf16[128,2688]{1,0:T(8,128)(2,1)} async-done(((bf16[2048,2688]{1,0:T(8,128)(2,1)}), bf16[128,2688]{1,0:T(8,128)(2,1)}) %reduce-scatter.2.cloned.1.call-update) | async-done | bytes 688144 | tf_op jit(solution)/shard_map/reduce_scatter | solution.py:287
  270.0 0.0 copy-done.3
  270.0 1.4 fusion.55
  271.4 0.0 copy-done.6
  271.4 2.7 fusion.11
  274.1 75.0 %all_to_all.29 = bf16[128,8,2688]{2,1,0:T(8,128)(2,1)} all-to-all(bf16[128,8,2688]{2,1,0:T(8,128)(2,1)S(1)} %fusion.11), channel_id=1, replica_groups=mesh['ctx'=8,'wide'=16] {'ctx','wide'}, dimensions={0} | all-to-all | bytes 11010048 | tf_op jit(solution)/shard_map/all_to_all | solution.py:295
  349.2 33.5 %fusion.8 = bf16[128,8,2688]{2,1,0:T(8,128)(2,1)} fusion(bf16[1,1856,2688]{2,1,0:T(8,128)(2,1)} %param.35, bf16[1,2688,1856]{1,2,0:T(8,128)(2,1)} %param.34, bf16[128,8,2688]{2,1,0:T(8,128)(2,1)} %all_to_all.29), kind=kOutput, calls=%fused_computation.8 | convolution fusion | flops 20443103232 | bytes 30965760 | tf_op jit(solution)/shard_map/dot_general | solution.py:302
  382.6 72.2 %all_to_all.30 = bf16[128,8,2688]{2,1,0:T(8,128)(2,1)S(1)} all-to-all(bf16[128,8,2688]{2,1,0:T(8,128)(2,1)} %fusion.8), channel_id=1, replica_groups=mesh['ctx'=8,'wide'=16] {'ctx','wide'}, dimensions={0} | all-to-all | bytes 11010048 | tf_op jit(solution)/shard_map/all_to_all | solution.py:303
  454.8 1.3 fusion.33
  456.1 0.0 copy-done.4
  456.1 2.3 fusion.45
  458.5 0.0 copy-done.1
  (13 shorter events, 0.1 us)
Async XLA Ops:
  6.5 5.8 %copy-start = (bf16[2688,64]{0,1:T(8,128)(2,1)S(1)}, bf16[2688,64]{0,1:T(8,128)(2,1)}, u32[]{:S(2)}) copy-start(bf16[2688,64]{0,1:T(8,128)(2,1)} %param.23) | copy-start | bytes 1032196
  6.5 31.2 %copy-start.5 = (bf16[2688,128]{1,0:T(8,128)(2,1)S(1)}, bf16[2688,128]{1,0:T(8,128)(2,1)}, u32[]{:S(2)}) copy-start(bf16[2688,128]{1,0:T(8,128)(2,1)} %param.22) | copy-start | bytes 2064388
  6.5 92.1 %all-gather.4.cloned.1.call-start = ((), (), s32[]{:S(2)}) async-start(), calls=%async_computation.4 | async-start | bytes 11698176 | tf_op jit(solution)/shard_map/all_gather | solution.py:263
  10.2 27.5 %collective-permute-start = (bf16[2688,128]{1,0:T(8,128)(2,1)}, bf16[2688,128]{1,0:T(8,128)(2,1)S(1)}, u32[]{:S(2)}, u32[]{:S(2)}) collective-permute-start(bf16[2688,128]{1,0:T(8,128)(2,1)} %param.22), channel_id=1, source_target_pairs={{0,1},{1,0},{2,3},{3,2},{4,5},{5,4},{6,7},{7,6},{8,9},{9,8},{10,11... | collective-permute-start | bytes 2064392 | tf_op jit(solution)/shard_map/ppermute | solution.py:248
  14.4 22.5 %all-to-all-start = ((f32[128,16,4]{0,2,1:T(4,128)}), f32[128,16,4]{0,2,1:T(4,128)S(1)}, u32[]{:S(2)}, u32[]{:S(2)}) async-start(f32[128,16,4]{0,2,1:T(4,128)} %bitcast), calls=%async_computation | async-start | bytes 65536 | tf_op jit(solution)/shard_map/all_to_all | solution.py:255
  21.9 137.4 %all-gather.6.cloned.1.call-start = ((), (), s32[]{:S(2)}) async-start(), calls=%async_computation.6 | async-start | bytes 1253376 | tf_op jit(solution)/shard_map/all_gather | solution.py:275
  111.7 5.8 %copy-start.2 = (bf16[2048,768]{1,0:T(8,128)(2,1)}, bf16[2048,768]{1,0:T(8,128)(2,1)S(1)}, u32[]{:S(2)}) copy-start(bf16[2048,768]{1,0:T(8,128)(2,1)S(1)} %fusion.48.proj_ref.gate_ref) | copy-start | bytes 9437188
  111.7 5.8 %collective-permute-start.1 = (bf16[8,512]{1,0:T(8,128)(2,1)S(1)}, bf16[8,512]{1,0:T(8,128)(2,1)S(1)}, u32[]{:S(2)}, u32[]{:S(2)}) collective-permute-start(bf16[8,512]{1,0:T(8,128)(2,1)S(1)} %slice.16), channel_id=1, source_target_pairs={{0,16},{16,32},{32,48},{48,64},{64,80},{80,96},{96,112},{1,17},{17... | collective-permute-start | bytes 24584 | tf_op jit(solution)/shard_map/ppermute | solution.py:27
  117.5 0.6 copy-start.7
  136.5 133.5 %reduce-scatter.2.cloned.1.call-start = ((), (), s32[]{:S(2)}) async-start(), calls=%async_computation.5 | async-start | bytes 11698176 | tf_op jit(solution)/shard_map/reduce_scatter | solution.py:287
  179.9 0.7 copy-start.8
  179.9 0.7 copy-start.9
  179.9 90.1 %copy-start.3 = (bf16[128,2688]{1,0:T(8,128)(2,1)S(1)}, bf16[128,2688]{1,0:T(8,128)(2,1)}, u32[]{:S(2)}) copy-start(bf16[128,2688]{1,0:T(8,128)(2,1)} %param.18) | copy-start | bytes 2064388
  179.9 91.5 %copy-start.6 = (f32[2688]{0:T(1024)S(1)}, f32[2688]{0:T(1024)}, u32[]{:S(2)}) copy-start(f32[2688]{0:T(1024)} %param.31) | copy-start | bytes 32260
  454.8 1.3 copy-start.4
  454.8 3.6 copy-start.1
Sparse Core Ops, SparseCore 0:
  10.3 88.3 all-gather.3
  136.6 22.6 all-gather.5
  180.1 89.8 reduce-scatter.1
